TPU v7x, 32 devices: a whole 2x2x4 slice. The times are simulated.
32 devices in a mesh: dp: 8 (over z, y), seq: 4 (over x, core).
Axes of the slice: x: 2, y: 2, z: 4, core: 2. Of those that a mesh axis runs over, the one named last changes fastest.
Arguments:
- tokens: bfloat16 [8, 512, 768], P('dp', 'seq'), may hold values from -6 to 6
- cotangent: bfloat16 [8, 512, 768], P('dp', 'seq'), may hold values from -6 to 6
- segment_ids: int32 [8, 512], P('dp', 'seq'), may hold values from 0 to 7, never falling along the last dimension, each value on 1 to 256 neighbouring positions
- pad_mask: int32 [8, 512], P('dp', 'seq'), may hold values 0 or 1
- routes: int32 [8, 512, 2], P('dp', 'seq'), may hold values from 0 to 3, all different within a row; in each aligned block of 128 rows (0 to 127, 128 to 255, ..., all dimensions but the last counted through in order) at most 96 rows name the same one
- gate_weights: float32 [8, 512, 2], P('dp', 'seq'), may hold values from 0.25 to 1
- gain_one: float32 [768], replicated, may hold values from 0.5 to 1.5
- w_qkv: bfloat16 [768, 2304], P(('dp', 'seq')), may hold values from -0.21875 to 0.21875
- w_attn: bfloat16 [768, 768], P(('dp', 'seq')), may hold values from -1.75 to 1.75
- rel_table: bfloat16 [12, 32], replicated, may hold values from -4 to 4
- gain_two: float32 [768], replicated, may hold values from 0.5 to 1.5
- w_expert_in: bfloat16 [4, 768, 3072], P(None, ('dp', 'seq')), may hold values from -0.21875 to 0.21875
- w_expert_out: bfloat16 [4, 3072, 768], P(None, ('dp', 'seq')), may hold values from -0.109375 to 0.109375
Outputs:
- output: bfloat16 [8, 512, 768], P('dp', 'seq')
- grad_tokens: float32 [8, 512, 768], P('dp', 'seq')
- grad_gain_one: float32 [768], replicated
- grad_w_qkv: float32 [768, 2304], P(('dp', 'seq'))
- grad_w_attn: float32 [768, 768], P(('dp', 'seq'))
- grad_rel_table: float32 [12, 32], replicated
- grad_gain_two: float32 [768], replicated
- grad_expert_in: float32 [4, 768, 3072], P(None, ('dp', 'seq'))
- grad_expert_out: float32 [4, 3072, 768], P(None, ('dp', 'seq'))
Inputs may be any that keep to these rules, and one draw needn't show every extreme that they name: `routes`: the two experts of a token differ. Among the rows of one device no expert is named more than 96 times, and in some device's rows one expert is named exactly 96 times. `segment_ids`: ids never fall along a sequence; a document has 1 to 256 positions, and one has exactly that many.
All inputs are finite; a program needn't handle non-finite values. No bound on the sum of `pad_mask` on one device may be relied on, other than what follows from the above.
Results may differ from a plain program's by a relative error of at most 0.011.
Values may be sent and summed in bfloat16 or wider, within the bound.
No kernel may reach another device: no remote copies, remote signals or barrier semaphores. Data moves between devices by JAX's collectives and lax.ppermute only.
A program may use at most 320 MiB of HBM per device.

v0:
```python
import math
import jax
import jax.numpy as jnp
import numpy as np
from jax import lax
from jax.sharding import PartitionSpec as P

BUCKETS = 32
MAX_DIST = 128
CAP = 96


def bucket_edges():
    exact_span = BUCKETS // 2
    distance = np.arange(1, 8 * MAX_DIST + 1)
    widened = np.maximum(distance, exact_span) / exact_span
    spread = exact_span + (np.log(widened) / np.log(MAX_DIST / exact_span) * exact_span).astype(
        np.int64
    )
    bucket_of = np.where(distance < exact_span, distance, np.minimum(spread, BUCKETS - 1))
    return np.array(
        [distance[np.argmax(bucket_of >= target)] for target in range(1, BUCKETS)], dtype=np.int32
    )


def norm_stats(values):
    factor = lax.rsqrt(jnp.mean(values * values, axis=-1, keepdims=True) + 1e-06)
    return (values * factor, factor)


def norm_back(grad_normed, scaled, factor, gain_vec):
    grad_scaled = grad_normed * gain_vec
    inner_mean = jnp.mean(grad_scaled * scaled, axis=-1, keepdims=True)
    return (factor * (grad_scaled - scaled * inner_mean), jnp.sum(grad_normed * scaled, axis=0))


def make_onehot(distance, edges_np):
    bucket_of = jnp.sum((distance[:, :, None] >= edges_np).astype(jnp.int32), axis=-1)
    return (bucket_of[:, :, None] == jnp.arange(BUCKETS, dtype=jnp.int32)).astype(jnp.bfloat16)


def block_bias(table_low, edges_np, distance):
    far_away = jnp.min(distance) >= int(edges_np[-1])

    def block_detailed(unused):
        return jnp.einsum(
            "qkb,hb->hqk",
            make_onehot(distance, edges_np),
            table_low,
            preferred_element_type=jnp.float32,
        )

    def block_constant(unused):
        last_col = table_low[:, BUCKETS - 1].astype(jnp.float32)
        return jnp.broadcast_to(last_col[:, None, None], (table_low.shape[0],) + distance.shape)

    return lax.cond(far_away, block_constant, block_detailed, 0)


def table_part(grad_low, edges_np, distance):
    far_away = jnp.min(distance) >= int(edges_np[-1])

    def table_detailed(unused):
        return jnp.einsum(
            "hqk,qkb->hb",
            grad_low,
            make_onehot(distance, edges_np),
            preferred_element_type=jnp.float32,
        )

    def table_constant(unused):
        totals = jnp.sum(grad_low, axis=(1, 2), dtype=jnp.float32)
        return totals[:, None] * (jnp.arange(BUCKETS) == BUCKETS - 1).astype(jnp.float32)

    return lax.cond(far_away, table_constant, table_detailed, 0)


def body(
    tokens,
    cotangent,
    segment_ids,
    pad_mask,
    routes,
    gate_weights,
    gain_one,
    w_qkv,
    w_attn,
    rel_table,
    gain_two,
    w_expert_in,
    w_expert_out,
):
    gathered = (
        lax.all_gather(w_qkv, ("dp", "seq"), axis=0, tiled=True),
        lax.all_gather(w_attn, ("dp", "seq"), axis=0, tiled=True),
        lax.all_gather(w_expert_in, ("dp", "seq"), axis=1, tiled=True),
        lax.all_gather(w_expert_out, ("dp", "seq"), axis=1, tiled=True),
    )
    full_qkv, full_attn, full_in, full_out = gathered
    inputs = tokens[0].astype(jnp.float32)
    row_count, model_width = inputs.shape
    head_count = rel_table.shape[0]
    head_size = model_width // head_count
    score_scale = head_size ** (-0.5)
    seg_local = segment_ids[0]
    seq_index = lax.axis_index("seq")
    length = row_count * lax.axis_size("seq")
    key_block = math.gcd(length, 512)
    query_pos = seq_index * row_count + jnp.arange(row_count, dtype=jnp.int32)
    block_count = ((seq_index + 1) * row_count + key_block - 1) // key_block
    edges_np = bucket_edges()
    scaled_one, factor_one = norm_stats(inputs)
    normed_one = (scaled_one * gain_one).astype(jnp.bfloat16)
    project = jnp.dot(normed_one, full_qkv, preferred_element_type=jnp.float32)
    queries = project[:, :model_width].astype(jnp.bfloat16)
    keys_local = project[:, model_width : 2 * model_width].astype(jnp.bfloat16)
    values_local = project[:, 2 * model_width :].astype(jnp.bfloat16)
    info_local = jnp.where(pad_mask[0] == 1, seg_local, -1)
    keys_all, values_all, info_all, seg_all = (
        lax.all_gather(keys_local, "seq", axis=0, tiled=True),
        lax.all_gather(values_local, "seq", axis=0, tiled=True),
        lax.all_gather(info_local, "seq", axis=0, tiled=True),
        lax.all_gather(seg_local, "seq", axis=0, tiled=True),
    )
    query_heads = queries.reshape(row_count, head_count, head_size)

    def block_scores(block_index):
        key_start = block_index * key_block
        key_heads = lax.dynamic_slice_in_dim(keys_all, key_start, key_block, 0).reshape(
            key_block, head_count, head_size
        )
        value_heads = lax.dynamic_slice_in_dim(values_all, key_start, key_block, 0).reshape(
            key_block, head_count, head_size
        )
        info_block = lax.dynamic_slice_in_dim(info_all, key_start, key_block, 0)
        key_pos = key_start + jnp.arange(key_block, dtype=jnp.int32)
        distance = query_pos[:, None] - key_pos[None, :]
        allowed = (distance >= 0) & ((info_block[None, :] == seg_local[:, None]) | (distance == 0))
        raw_scores = (
            jnp.einsum("qhd,khd->hqk", query_heads, key_heads, preferred_element_type=jnp.float32)
            * score_scale
        )
        raw_scores = raw_scores + block_bias(rel_table, edges_np, distance)
        return (
            jnp.where(allowed[None], raw_scores, -1e30),
            allowed[None],
            key_heads,
            value_heads,
            distance,
            key_start,
        )

    def max_step(block_index, running):
        top_score, row_total = running
        pieces = block_scores(block_index)
        new_top = jnp.maximum(top_score, jnp.max(pieces[0], axis=-1))
        exponent = jnp.where(pieces[1], jnp.exp(pieces[0] - new_top[:, :, None]), 0.0)
        return (new_top, row_total * jnp.exp(top_score - new_top) + jnp.sum(exponent, axis=-1))

    start_top = jnp.full((head_count, row_count), -1e30, jnp.float32)
    start_total = jnp.zeros((head_count, row_count), jnp.float32)
    top_score, row_total = lax.fori_loop(0, block_count, max_step, (start_top, start_total))
    log_total = top_score + jnp.log(row_total)

    def out_step(block_index, mixed_acc):
        pieces = block_scores(block_index)
        prob_low = jnp.where(pieces[1], jnp.exp(pieces[0] - log_total[:, :, None]), 0.0).astype(
            jnp.bfloat16
        )
        return mixed_acc + jnp.einsum(
            "hqk,khd->qhd", prob_low, pieces[3], preferred_element_type=jnp.float32
        )

    mixed_full = lax.fori_loop(
        0, block_count, out_step, jnp.zeros((row_count, head_count, head_size), jnp.float32)
    )
    mixed_low = mixed_full.reshape(row_count, model_width).astype(jnp.bfloat16)
    hidden_one = inputs + jnp.dot(mixed_low, full_attn, preferred_element_type=jnp.float32)
    scaled_two, factor_two = norm_stats(hidden_one)
    normed_two = (scaled_two * gain_two).astype(jnp.bfloat16)
    route_local = routes[0]
    expert_count = w_expert_in.shape[0]
    top_count = route_local.shape[1]
    flat_routes = route_local.reshape(-1)
    expert_hot = (flat_routes[:, None] == jnp.arange(expert_count, dtype=jnp.int32)).astype(
        jnp.int32
    )
    earlier = jnp.cumsum(expert_hot, axis=0) - expert_hot
    slot_index = jnp.sum(earlier * expert_hot, axis=1)
    slot_float = (
        (slot_index[:, None] == jnp.arange(CAP, dtype=jnp.int32))
        .astype(jnp.float32)
        .reshape(row_count, top_count, CAP)
    )
    expert_float = expert_hot.astype(jnp.float32).reshape(row_count, top_count, expert_count)
    dispatch = jnp.einsum(
        "tke,tkc->ect",
        expert_float.astype(jnp.bfloat16),
        slot_float.astype(jnp.bfloat16),
        preferred_element_type=jnp.float32,
    ).astype(jnp.bfloat16)
    slot_gate = jnp.einsum(
        "tke,tkc,tk->ec", expert_float, slot_float, gate_weights[0], precision=lax.Precision.HIGHEST
    )
    entered = jnp.einsum(
        "ect,td->ecd", dispatch, normed_two, preferred_element_type=jnp.float32
    ).astype(jnp.bfloat16)
    pre_act = jnp.einsum("ecd,edf->ecf", entered, full_in, preferred_element_type=jnp.float32)
    active = jax.nn.gelu(pre_act).astype(jnp.bfloat16)
    result = jnp.einsum("ecf,efd->ecd", active, full_out, preferred_element_type=jnp.float32)
    expert_low = (slot_gate[:, :, None] * result).astype(jnp.bfloat16)
    combined = jnp.einsum("ect,ecd->td", dispatch, expert_low, preferred_element_type=jnp.float32)
    output = (hidden_one + combined).astype(jnp.bfloat16)
    regathered = (
        lax.all_gather(w_qkv, ("dp", "seq"), axis=0, tiled=True),
        lax.all_gather(w_attn, ("dp", "seq"), axis=0, tiled=True),
        lax.all_gather(w_expert_in, ("dp", "seq"), axis=1, tiled=True),
        lax.all_gather(w_expert_out, ("dp", "seq"), axis=1, tiled=True),
    )
    back_qkv, back_attn, back_in, back_out = regathered
    grad_out_low = cotangent[0]
    grad_slots = jnp.einsum(
        "ect,td->ecd", dispatch, grad_out_low, preferred_element_type=jnp.float32
    )
    grad_result = (slot_gate[:, :, None] * grad_slots).astype(jnp.bfloat16)
    grad_w_out = jnp.einsum("ecf,ecd->efd", active, grad_result, preferred_element_type=jnp.float32)
    grad_active = jnp.einsum(
        "ecd,efd->ecf", grad_result, back_out, preferred_element_type=jnp.float32
    )
    unused_value, gelu_pull = jax.vjp(jax.nn.gelu, pre_act)
    grad_pre = gelu_pull(grad_active)[0].astype(jnp.bfloat16)
    grad_w_in = jnp.einsum("ecd,ecf->edf", entered, grad_pre, preferred_element_type=jnp.float32)
    grad_entered = jnp.einsum(
        "ecf,edf->ecd", grad_pre, back_in, preferred_element_type=jnp.float32
    ).astype(jnp.bfloat16)
    grad_normed_two = jnp.einsum(
        "ect,ecd->td", dispatch, grad_entered, preferred_element_type=jnp.float32
    )
    grad_hidden_norm, grad_gain_two = norm_back(grad_normed_two, scaled_two, factor_two, gain_two)
    grad_hidden = grad_out_low.astype(jnp.float32) + grad_hidden_norm
    branch_low = grad_hidden.astype(jnp.bfloat16)
    grad_w_attn = lax.dot_general(
        mixed_low, branch_low, (((0,), (0,)), ((), ())), preferred_element_type=jnp.float32
    )
    grad_mixed = lax.dot_general(
        branch_low, back_attn, (((1,), (1,)), ((), ())), preferred_element_type=jnp.float32
    ).astype(jnp.bfloat16)
    grad_mixed_heads = grad_mixed.reshape(row_count, head_count, head_size)
    row_delta = jnp.sum(grad_mixed_heads.astype(jnp.float32) * mixed_full, axis=-1).T

    def score_grads(pieces):
        prob_full = jnp.where(pieces[1], jnp.exp(pieces[0] - log_total[:, :, None]), 0.0)
        grad_prob = jnp.einsum(
            "qhd,khd->hqk", grad_mixed_heads, pieces[3], preferred_element_type=jnp.float32
        )
        grad_score = (prob_full * (grad_prob - row_delta[:, :, None])).astype(jnp.bfloat16)
        return (prob_full.astype(jnp.bfloat16), grad_score)

    start_query = jnp.zeros((row_count, head_count, head_size), jnp.float32)
    start_table = jnp.zeros((head_count, BUCKETS), jnp.float32)

    def back_step(block_index, running):
        grad_query, grad_key_all, grad_value_all, grad_table = running
        pieces = block_scores(block_index)
        prob_low, grad_score = score_grads(pieces)
        grad_query = (
            grad_query
            + jnp.einsum("hqk,khd->qhd", grad_score, pieces[2], preferred_element_type=jnp.float32)
            * score_scale
        )
        key_part = (
            jnp.einsum("hqk,qhd->khd", grad_score, query_heads, preferred_element_type=jnp.float32)
            * score_scale
        ).reshape(key_block, model_width)
        value_part = jnp.einsum(
            "hqk,qhd->khd", prob_low, grad_mixed_heads, preferred_element_type=jnp.float32
        ).reshape(key_block, model_width)
        grad_key_all = lax.dynamic_update_slice_in_dim(grad_key_all, key_part, pieces[5], 0)
        grad_value_all = lax.dynamic_update_slice_in_dim(grad_value_all, value_part, pieces[5], 0)
        grad_table = grad_table + table_part(grad_score, edges_np, pieces[4])
        return (grad_query, grad_key_all, grad_value_all, grad_table)

    start_back = (
        start_query,
        jnp.zeros((length, model_width), jnp.float32),
        jnp.zeros((length, model_width), jnp.float32),
        start_table,
    )
    grad_query, grad_key_all, grad_value_all, grad_table = lax.fori_loop(
        0, block_count, back_step, start_back
    )
    grad_keys, grad_values = (
        lax.psum_scatter(
            grad_key_all.astype(jnp.bfloat16), "seq", scatter_dimension=0, tiled=True
        ).astype(jnp.float32),
        lax.psum_scatter(
            grad_value_all.astype(jnp.bfloat16), "seq", scatter_dimension=0, tiled=True
        ).astype(jnp.float32),
    )
    grad_proj = jnp.concatenate(
        [
            grad_query.reshape(row_count, model_width).astype(jnp.bfloat16),
            grad_keys.astype(jnp.bfloat16),
            grad_values.astype(jnp.bfloat16),
        ],
        axis=1,
    )
    grad_w_qkv = lax.dot_general(
        normed_one, grad_proj, (((0,), (0,)), ((), ())), preferred_element_type=jnp.float32
    )
    grad_normed_one = lax.dot_general(
        grad_proj, back_qkv, (((1,), (1,)), ((), ())), preferred_element_type=jnp.float32
    )
    grad_input_norm, grad_gain_one = norm_back(grad_normed_one, scaled_one, factor_one, gain_one)
    grad_inputs = grad_hidden + grad_input_norm
    table_total, gain_one_total, gain_two_total = lax.psum(
        (grad_table, grad_gain_one, grad_gain_two), ("dp", "seq")
    )
    shares = (
        lax.psum_scatter(grad_w_qkv, ("dp", "seq"), scatter_dimension=0, tiled=True),
        lax.psum_scatter(grad_w_attn, ("dp", "seq"), scatter_dimension=0, tiled=True),
        lax.psum_scatter(grad_w_in, ("dp", "seq"), scatter_dimension=1, tiled=True),
        lax.psum_scatter(grad_w_out, ("dp", "seq"), scatter_dimension=1, tiled=True),
    )
    return (
        output[None],
        grad_inputs[None],
        gain_one_total,
        shares[0],
        shares[1],
        table_total,
        gain_two_total,
        shares[2],
        shares[3],
    )


def solution(mesh):
    return jax.shard_map(
        body,
        mesh=mesh,
        in_specs=(
            P("dp", "seq", None),
            P("dp", "seq", None),
            P("dp", "seq"),
            P("dp", "seq"),
            P("dp", "seq", None),
            P("dp", "seq", None),
            P(),
            P(("dp", "seq"), None),
            P(("dp", "seq"), None),
            P(),
            P(),
            P(None, ("dp", "seq"), None),
            P(None, ("dp", "seq"), None),
        ),
        out_specs=(
            P("dp", "seq", None),
            P("dp", "seq", None),
            P(),
            P(("dp", "seq"), None),
            P(("dp", "seq"), None),
            P(),
            P(),
            P(None, ("dp", "seq"), None),
            P(None, ("dp", "seq"), None),
        ),
        check_vma=False,
    )
```

profile of v0, /device:TPU:0, one launch (start us, length us, event | category | flops | bytes accessed | tf_op | source)
XLA Modules:
  0.0 1434.7 jit_solution(6802587693438444505)
XLA Ops:
  25.1 48.6 %all-gather.6.cloned.1.call-done = bf16[768,2304]{1,0:T(8,128)(2,1)} async-done(((bf16[24,2304]{1,0:T(8,128)(2,1)}), bf16[768,2304]{1,0:T(8,128)(2,1)}) %all-gather.6.cloned.1.call-update) | async-done | bytes 3538960 | tf_op jit(solution)/shard_map/all_gather | solution.py:94
  76.6 8.6 all_gather.27
  86.5 8.7 all_gather.28
  97.0 10.8 while.44
  108.5 12.9 while.45
  110.2 6.7 conditional.21
  121.5 8.0 all-gather.8.cloned.1.call-done
  132.5 123.6 %all-gather.12.cloned.1.call-done = bf16[4,3072,768]{2,1,0:T(8,128)(2,1)} async-done(((bf16[4,96,768]{2,1,0:T(8,128)(2,1)}), bf16[4,3072,768]{2,1,0:T(8,128)(2,1)}) %all-gather.12.cloned.1.call-update) | async-done | bytes 18874384 | tf_op jit(solution)/shard_map/all_gather | solution.py:97
  256.1 14.2 fusion.98
  270.3 111.4 %all-gather.10.cloned.1.call-done = bf16[4,768,3072]{2,1,0:T(8,128)(2,1)} async-done(((bf16[4,24,3072]{2,1,0:T(8,128)(2,1)}), bf16[4,768,3072]{2,1,0:T(8,128)(2,1)}) %all-gather.10.cloned.1.call-update) | async-done | bytes 18874384 | tf_op jit(solution)/shard_map/all_gather | solution.py:96
  381.7 11.7 fusion.46
  393.4 14.6 %multiply_reduce_fusion = (f32[768]{0:T(1024)}, f32[128]{0:T(128)S(1)}, f32[128,768]{1,0:T(8,128)}) fusion(f32[128,768]{1,0:T(8,128)S(1)} %get-tuple-element.749, f32[128]{0:T(128)S(1)} %add_rsqrt_fusion, f32[768]{0:T(1024)S(1)} %copy-done.44, bf16[4,96,128]{2,1,0:T(8,128)(2,1)S(1)} %copy-done.25, bf16[4,96,3072]{2,1,0:T(8,128)(2,1)S(1)} %get-tuple-element.750, ...), kind=kOutput, calls=%fused_computation.122 | convolution fusion | flops 1888320640 | bytes 22125568 | tf_op jit(solution)/shard_map/ect,ecd->td/dot_general | solution.py:236
  416.3 23.6 %while.46 = (s32[]{:T(128)}, f32[128,12,64]{0,2,1:T(8,128)}, bf16[512,768]{0,1:T(8,128)(2,1)}, bf16[512,768]{0,1:T(8,128)(2,1)}, f32[12,32]{1,0:T(8,128)S(1)}, /...) while((s32[]{:T(128)}, f32[128,12,64]{0,2,1:T(8,128)}, ...), condition=%wide.region_30.31_spmd.clone.clone, body=%wide.region_21.30_spmd.sunk.clone.clone.sunk | while | flops 628818944 | bytes 50517476 | solution.py:289
  432.2 7.6 conditional.23
  446.9 17.0 %reduce-scatter.21.cloned.1.call-done = bf16[128,768]{1,0:T(8,128)(2,1)} async-done(((bf16[512,768]{1,0:T(8,128)(2,1)}), bf16[128,768]{1,0:T(8,128)(2,1)}) %reduce-scatter.21.cloned.1.call-update) | async-done | bytes 196624
  465.0 25.3 %reduce-scatter.19.cloned.1.call-done = bf16[128,768]{1,0:T(8,128)(2,1)} async-done(((bf16[512,768]{1,0:T(8,128)(2,1)}), bf16[128,768]{1,0:T(8,128)(2,1)}) %reduce-scatter.19.cloned.1.call-update) | async-done | bytes 196624
  497.3 15.2 %fusion.99 = f32[4,768,3072]{2,1,0:T(8,128)} fusion(bf16[4,96,768]{2,1,0:T(8,128)(2,1)S(1)} %copy-done.20, bf16[4,96,3072]{2,1,0:T(8,128)(2,1)S(1)} %copy-done.10), kind=kOutput, calls=%fused_computation.168 | convolution fusion | flops 1811939328 | bytes 40697856 | tf_op jit(solution)/shard_map/ecd,ecf->edf/dot_general | solution.py:232
  513.6 17.7 %fusion.95 = f32[4,3072,768]{2,1,0:T(8,128)} fusion(bf16[4,96,768]{2,1,0:T(8,128)(2,1)S(1)} %copy-done.18, f32[4,96,3072]{2,1,0:T(8,128)} %get-tuple-element.751), kind=kOutput, calls=%fused_computation.164 | convolution fusion | flops 1822556160 | bytes 43057152 | tf_op jit(solution)/shard_map/ecf,ecd->efd/dot_general | solution.py:226
  532.3 10.7 fusion.55
  546.8 39.7 %all-reduce = (f32[768]{0:T(1024)}, f32[12,32]{1,0:T(8,128)}, f32[768]{0:T(1024)}) all-reduce(f32[768]{0:T(1024)S(1)} %get-tuple-element.658, f32[12,32]{1,0:T(8,128)S(1)} %copy-done.35, f32[768]{0:T(1024)S(1)} %copy-done.45), channel_id=1, replica_groups=mesh['dp'=8,'seq'=4] {'dp','seq'}, use_global_device_ids=true, to_apply=%region_35.36 | all-reduce | flops 1920 | bytes 15360 | tf_op jit(solution)/shard_map/psum | solution.py:316
  587.4 7.9 reduce-scatter.13.cloned.1.call-done
  595.3 125.1 %reduce-scatter.11.cloned.1.call-done = f32[24,2304]{1,0:T(8,128)} async-done(((f32[768,2304]{1,0:T(8,128)}), f32[24,2304]{1,0:T(8,128)}) %reduce-scatter.11.cloned.1.call-update) | async-done | bytes 221200 | tf_op jit(solution)/shard_map/reduce_scatter | solution.py:320
  720.4 353.4 %reduce-scatter.15.cloned.1.call-done = f32[4,24,3072]{2,1,0:T(8,128)} async-done(((f32[4,768,3072]{2,1,0:T(8,128)}), f32[4,24,3072]{2,1,0:T(8,128)}) %reduce-scatter.15.cloned.1.call-update) | async-done | bytes 1179664 | tf_op jit(solution)/shard_map/reduce_scatter | solution.py:322
  1073.8 353.9 %reduce-scatter.17.cloned.1.call-done = f32[4,96,768]{2,1,0:T(8,128)} async-done(((f32[4,3072,768]{2,1,0:T(8,128)}), f32[4,96,768]{2,1,0:T(8,128)}) %reduce-scatter.17.cloned.1.call-update) | async-done | bytes 1179664 | tf_op jit(solution)/shard_map/reduce_scatter | solution.py:323
  (217 shorter events, 110.9 us)
Async XLA Ops:
  7.2 66.6 %copy-start.15 = (bf16[1,128,768]{2,1,0:T(8,128)(2,1)S(1)}, bf16[1,128,768]{2,1,0:T(8,128)(2,1)}, u32[]{:S(2)}) copy-start(bf16[1,128,768]{2,1,0:T(8,128)(2,1)} %param.28) | copy-start | bytes 589828
  7.2 66.6 %copy-start.40 = (f32[768]{0:T(1024)S(1)}, f32[768]{0:T(1024)}, u32[]{:S(2)}) copy-start(f32[768]{0:T(1024)} %param.34) | copy-start | bytes 9220
  7.2 66.6 %all-gather.6.cloned.1.call-start = ((), (), s32[]{:S(2)}) async-start(), calls=%async_computation.6 | async-start | bytes 3649536 | tf_op jit(solution)/shard_map/all_gather | solution.py:94
  7.9 121.6 %all-gather.8.cloned.1.call-start = ((), (), s32[]{:S(2)}) async-start(), calls=%async_computation.7 | async-start | bytes 1216512 | tf_op jit(solution)/shard_map/all_gather | solution.py:95
  8.7 247.4 %all-gather.12.cloned.1.call-start = ((), (), s32[]{:S(2)}) async-start(), calls=%async_computation.9 | async-start | bytes 19464192 | tf_op jit(solution)/shard_map/all_gather | solution.py:97
  9.4 372.3 %all-gather.10.cloned.1.call-start = ((), (), s32[]{:S(2)}) async-start(), calls=%async_computation.8 | async-start | bytes 19464192 | tf_op jit(solution)/shard_map/all_gather | solution.py:96
  10.0 453.9 %reduce-scatter.21.cloned.1.call-start = ((), (), s32[]{:S(2)}) async-start(), calls=%async_computation.15 | async-start | bytes 983040
  14.5 62.1 %copy-start.23 = (bf16[4,96,128]{2,1,0:T(8,128)(2,1)}, bf16[4,96,128]{2,1,0:T(8,128)(2,1)S(1)}, u32[]{:S(2)}) copy-start(bf16[4,96,128]{2,1,0:T(8,128)(2,1)S(1)} %copy.119) | copy-start | bytes 294916
  22.0 54.6 %copy-start.48 = (f32[4,96]{1,0:T(4,128)}, f32[4,96]{1,0:T(4,128)S(1)}, u32[]{:S(2)}) copy-start(f32[4,96]{1,0:T(4,128)S(1)} %convolution_bitcast_fusion) | copy-start | bytes 4612
  23.1 53.5 %copy-start.46 = (f32[128]{0:T(128)}, f32[128]{0:T(128)S(1)}, u32[]{:S(2)}) copy-start(f32[128]{0:T(128)S(1)} %add_rsqrt_fusion.1) | copy-start | bytes 1540
  121.4 148.9 %copy-start.38 = (f32[12,128]{1,0:T(8,128)}, f32[12,128]{1,0:T(8,128)S(1)}, u32[]{:S(2)}) copy-start(f32[12,128]{1,0:T(8,128)S(1)} %get-tuple-element.1187) | copy-start | bytes 18436
  121.5 134.6 %copy-start.17 = (bf16[4,96,768]{2,1,0:T(8,128)(2,1)S(1)}, bf16[4,96,768]{2,1,0:T(8,128)(2,1)}, u32[]{:S(2)}) copy-start(bf16[4,96,768]{2,1,0:T(8,128)(2,1)} %fusion.47) | copy-start | bytes 1769476
  121.5 148.8 %copy-start.21 = (bf16[128,12,64]{0,2,1:T(8,128)(2,1)}, bf16[128,12,64]{0,2,1:T(8,128)(2,1)S(1)}, u32[]{:S(2)}) copy-start(bf16[128,12,64]{0,2,1:T(8,128)(2,1)S(1)} %convert_element_type.181) | copy-start | bytes 589828
  131.3 276.7 %copy-start.13 = (f32[128,768]{1,0:T(8,128)}, f32[128,768]{1,0:T(8,128)S(1)}, u32[]{:S(2)}) copy-start(f32[128,768]{1,0:T(8,128)S(1)} %get-tuple-element.749) | copy-start | bytes 1179652
  270.3 123.1 %copy-start.25 = (bf16[4,96,128]{2,1,0:T(8,128)(2,1)S(1)}, bf16[4,96,128]{2,1,0:T(8,128)(2,1)}, u32[]{:S(2)}) copy-start(bf16[4,96,128]{2,1,0:T(8,128)(2,1)} %copy-done.23) | copy-start | bytes 294916
  270.3 123.1 %copy-start.44 = (f32[768]{0:T(1024)S(1)}, f32[768]{0:T(1024)}, u32[]{:S(2)}) copy-start(f32[768]{0:T(1024)} %param.38) | copy-start | bytes 9220
  442.3 48.0 %reduce-scatter.19.cloned.1.call-start = ((), (), s32[]{:S(2)}) async-start(), calls=%async_computation.14 | async-start | bytes 983040
  444.6 46.7 %copy-start.16 = (bf16[1,128,768]{2,1,0:T(8,128)(2,1)S(1)}, bf16[1,128,768]{2,1,0:T(8,128)(2,1)}, u32[]{:S(2)}) copy-start(bf16[1,128,768]{2,1,0:T(8,128)(2,1)} %param.28) | copy-start | bytes 589828
  444.6 46.7 %copy-start.41 = (f32[768]{0:T(1024)S(1)}, f32[768]{0:T(1024)}, u32[]{:S(2)}) copy-start(f32[768]{0:T(1024)} %param.34) | copy-start | bytes 9220
  444.7 150.6 %reduce-scatter.13.cloned.1.call-start = ((), (), s32[]{:S(2)}) async-start(), calls=%async_computation.11 | async-start | bytes 2433024 | tf_op jit(solution)/shard_map/reduce_scatter | solution.py:321
  446.6 273.8 %reduce-scatter.11.cloned.1.call-start = ((), (), s32[]{:S(2)}) async-start(), calls=%async_computation.10 | async-start | bytes 7299072 | tf_op jit(solution)/shard_map/reduce_scatter | solution.py:320
  446.9 48.7 %copy-start.31 = (bf16[128,12,64]{0,2,1:T(8,128)(2,1)}, bf16[128,12,64]{0,2,1:T(8,128)(2,1)S(1)}, u32[]{:S(2)}) copy-start(bf16[128,12,64]{0,2,1:T(8,128)(2,1)S(1)} %convert_element_type.204) | copy-start | bytes 589828
  495.6 578.2 %reduce-scatter.15.cloned.1.call-start = ((), (), s32[]{:S(2)}) async-start(), calls=%async_computation.12 | async-start | bytes 38928384 | tf_op jit(solution)/shard_map/reduce_scatter | solution.py:322
  512.5 915.2 %reduce-scatter.17.cloned.1.call-start = ((), (), s32[]{:S(2)}) async-start(), calls=%async_computation.13 | async-start | bytes 38928384 | tf_op jit(solution)/shard_map/reduce_scatter | solution.py:323
  (36 other events, 267.2 us)
Sparse Core Ops, SparseCore 0:
  10.9 62.8 all-gather.5
  76.7 52.8 all-gather.7
  132.5 123.5 all-gather.11
  258.9 122.7 all-gather.9
  442.4 21.4 reduce-scatter.20
  467.0 23.2 reduce-scatter.18
  496.1 99.1 reduce-scatter.12
  602.5 117.8 reduce-scatter.10
  727.4 346.3 reduce-scatter.14
  1081.8 345.9 reduce-scatter.16
where the time goes:
time: 1440 us; the launch traced here: 1430 us
  waiting for transfers between devices  1180 us (82%)
  matrix products  125 us (9%)
  blocking collectives  63 us (4%)
  local copies, waits for them, and re-layouts  31.1 us (2%)
  other arithmetic  20 us (1%)
  between operations  14.8 us (1%)
    reduce_scatter x1, waiting for transfers between devices, body(): lax.psum_scatter(grad_w_out, ('dp', 'seq'), scatter_dimension=1, tiled=True)  354 us
    reduce_scatter x1, waiting for transfers between devices, body(): lax.psum_scatter(grad_w_in, ('dp', 'seq'), scatter_dimension=1, tiled=True)  353 us
    reduce_scatter x1, waiting for transfers between devices, body(): lax.psum_scatter(grad_w_qkv, ('dp', 'seq'), scatter_dimension=0, tiled=True)  125 us
    all_gather x1, waiting for transfers between devices, body(): lax.all_gather(w_expert_out, ('dp', 'seq'), axis=1, tiled=True)  124 us
    all_gather x1, waiting for transfers between devices, body(): lax.all_gather(w_expert_in, ('dp', 'seq'), axis=1, tiled=True)  111 us
    all_gather x1, waiting for transfers between devices, body(): lax.all_gather(w_qkv, ('dp', 'seq'), axis=0, tiled=True)  48.6 us
    unnamed x12, waiting for transfers between devices  45 us
    psum x1, blocking collectives, body(): lax.psum((grad_table, grad_gain_one, grad_gain_two), ('dp', 'seq'))  39.7 us
  transfers between devices with their start and end apart: 10, of which 10 were waited for; matrix products, arithmetic and copies ran while one was open for 8% of the time, Pallas kernels for 0%

commit v1 on v0

--- a/solution.py
+++ b/solution.py
@@ -314,7 +314,7 @@
     grad_input_norm, grad_gain_one = norm_back(grad_normed_one, scaled_one, factor_one, gain_one)
     grad_inputs = grad_hidden + grad_input_norm
     table_total, gain_one_total, gain_two_total = lax.psum(
-        (grad_table, grad_gain_one, grad_gain_two), ("dp", "seq")
+        lax.psum((grad_table, grad_gain_one, grad_gain_two), axis_name="seq"), axis_name="dp"
     )
     shares = (
         lax.psum_scatter(grad_w_qkv, ("dp", "seq"), scatter_dimension=0, tiled=True),

time: 1440 us -> 1440 us (level)
    psum x1 -> x2, blocking collectives: 39.7 us -> 48.6 us  [the longest x1 37.7 us: body(): lax.psum(lax.psum((grad_table, grad_gain_one, grad_gain_two), axis_name='...]
  transfers between devices with their start and end apart: 10 -> 10, of which waited for: 10 -> 9; matrix products, arithmetic and copies ran while one was open for 8% -> 8% of each run, Pallas kernels for 0% -> 0%
where the time goes in v1:
time: 1440 us; the launch traced here: 1430 us
  waiting for transfers between devices  1170 us (81%)
  matrix products  125 us (9%)
  blocking collectives  71.9 us (5%)
  local copies, waits for them, and re-layouts  31.1 us (2%)
  other arithmetic  19.9 us (1%)
  between operations  14.8 us (1%)
    reduce_scatter x1, waiting for transfers between devices, body(): lax.psum_scatter(grad_w_out, ('dp', 'seq'), scatter_dimension=1, tiled=True)  354 us
    reduce_scatter x1, waiting for transfers between devices, body(): lax.psum_scatter(grad_w_in, ('dp', 'seq'), scatter_dimension=1, tiled=True)  353 us
    reduce_scatter x1, waiting for transfers between devices, body(): lax.psum_scatter(grad_w_qkv, ('dp', 'seq'), scatter_dimension=0, tiled=True)  124 us
    all_gather x1, waiting for transfers between devices, body(): lax.all_gather(w_expert_out, ('dp', 'seq'), axis=1, tiled=True)  124 us
    all_gather x1, waiting for transfers between devices, body(): lax.all_gather(w_expert_in, ('dp', 'seq'), axis=1, tiled=True)  111 us
    all_gather x1, waiting for transfers between devices, body(): lax.all_gather(w_qkv, ('dp', 'seq'), axis=0, tiled=True)  48.6 us
    unnamed x12, waiting for transfers between devices  45 us
    psum x1, blocking collectives, body(): lax.psum(lax.psum((grad_table, grad_gain_one, grad_gain_two), axis_name='...  37.7 us
  transfers between devices with their start and end apart: 10, of which 9 were waited for; matrix products, arithmetic and copies ran while one was open for 8% of the time, Pallas kernels for 0%

profile of v1, /device:TPU:0, one launch (start us, length us, event | category | flops | bytes accessed | tf_op | source)
XLA Modules:
  0.0 1434.3 jit_solution(13954265193933379)
XLA Ops:
  25.1 48.6 %all-gather.6.cloned.1.call-done = bf16[768,2304]{1,0:T(8,128)(2,1)} async-done(((bf16[24,2304]{1,0:T(8,128)(2,1)}), bf16[768,2304]{1,0:T(8,128)(2,1)}) %all-gather.6.cloned.1.call-update) | async-done | bytes 3538960 | tf_op jit(solution)/shard_map/all_gather | solution.py:94
  76.6 8.6 all_gather.27
  86.5 8.7 all_gather.28
  97.0 10.8 while.44
  108.5 12.9 while.45
  110.2 6.7 conditional.21
  121.5 8.0 all-gather.8.cloned.1.call-done
  132.5 123.6 %all-gather.12.cloned.1.call-done = bf16[4,3072,768]{2,1,0:T(8,128)(2,1)} async-done(((bf16[4,96,768]{2,1,0:T(8,128)(2,1)}), bf16[4,3072,768]{2,1,0:T(8,128)(2,1)}) %all-gather.12.cloned.1.call-update) | async-done | bytes 18874384 | tf_op jit(solution)/shard_map/all_gather | solution.py:97
  256.1 14.2 fusion.98
  270.3 111.4 %all-gather.10.cloned.1.call-done = bf16[4,768,3072]{2,1,0:T(8,128)(2,1)} async-done(((bf16[4,24,3072]{2,1,0:T(8,128)(2,1)}), bf16[4,768,3072]{2,1,0:T(8,128)(2,1)}) %all-gather.10.cloned.1.call-update) | async-done | bytes 18874384 | tf_op jit(solution)/shard_map/all_gather | solution.py:96
  381.7 11.7 fusion.46
  393.4 14.6 %multiply_reduce_fusion = (f32[768]{0:T(1024)}, f32[128]{0:T(128)S(1)}, f32[128,768]{1,0:T(8,128)}) fusion(f32[128,768]{1,0:T(8,128)S(1)} %get-tuple-element.752, f32[128]{0:T(128)S(1)} %add_rsqrt_fusion, f32[768]{0:T(1024)S(1)} %copy-done.44, bf16[4,96,128]{2,1,0:T(8,128)(2,1)S(1)} %copy-done.25, bf16[4,96,3072]{2,1,0:T(8,128)(2,1)S(1)} %get-tuple-element.753, ...), kind=kOutput, calls=%fused_computation.122 | convolution fusion | flops 1888320640 | bytes 22125568 | tf_op jit(solution)/shard_map/ect,ecd->td/dot_general | solution.py:236
  416.3 23.3 %while.46 = (s32[]{:T(128)}, f32[128,12,64]{0,2,1:T(8,128)}, bf16[512,768]{0,1:T(8,128)(2,1)}, bf16[512,768]{0,1:T(8,128)(2,1)}, f32[12,32]{1,0:T(8,128)S(1)}, /...) while((s32[]{:T(128)}, f32[128,12,64]{0,2,1:T(8,128)}, ...), condition=%wide.region_30.31_spmd.clone.clone, body=%wide.region_21.30_spmd.sunk.clone.clone.sunk | while | flops 628818944 | bytes 50517476 | solution.py:289
  431.9 7.6 conditional.23
  446.6 17.0 %reduce-scatter.21.cloned.1.call-done = bf16[128,768]{1,0:T(8,128)(2,1)} async-done(((bf16[512,768]{1,0:T(8,128)(2,1)}), bf16[128,768]{1,0:T(8,128)(2,1)}) %reduce-scatter.21.cloned.1.call-update) | async-done | bytes 196624
  464.6 25.3 %reduce-scatter.19.cloned.1.call-done = bf16[128,768]{1,0:T(8,128)(2,1)} async-done(((bf16[512,768]{1,0:T(8,128)(2,1)}), bf16[128,768]{1,0:T(8,128)(2,1)}) %reduce-scatter.19.cloned.1.call-update) | async-done | bytes 196624
  497.0 15.2 %fusion.99 = f32[4,768,3072]{2,1,0:T(8,128)} fusion(bf16[4,96,768]{2,1,0:T(8,128)(2,1)S(1)} %copy-done.20, bf16[4,96,3072]{2,1,0:T(8,128)(2,1)S(1)} %copy-done.10), kind=kOutput, calls=%fused_computation.168 | convolution fusion | flops 1811939328 | bytes 40697856 | tf_op jit(solution)/shard_map/ecd,ecf->edf/dot_general | solution.py:232
  513.3 17.7 %fusion.95 = f32[4,3072,768]{2,1,0:T(8,128)} fusion(bf16[4,96,768]{2,1,0:T(8,128)(2,1)S(1)} %copy-done.18, f32[4,96,3072]{2,1,0:T(8,128)} %get-tuple-element.754), kind=kOutput, calls=%fused_computation.164 | convolution fusion | flops 1822556160 | bytes 43057152 | tf_op jit(solution)/shard_map/ecf,ecd->efd/dot_general | solution.py:226
  532.0 10.7 fusion.55
  546.4 10.9 all-reduce.1
  557.4 37.7 %all-reduce = (f32[768]{0:T(1024)}, f32[12,32]{1,0:T(8,128)}, f32[768]{0:T(1024)}) all-reduce(f32[768]{0:T(1024)S(1)} %get-tuple-element.737, f32[12,32]{1,0:T(8,128)S(1)} %get-tuple-element.738, f32[768]{0:T(1024)S(1)} %get-tuple-element.739), channel_id=1, replica_groups=mesh['dp'=8,'seq'=4] {'dp'}, use_global_device_ids=true, to_apply=%region_36.37 | all-reduce | flops 1920 | bytes 15360 | tf_op jit(solution)/shard_map/psum | solution.py:316
  596.0 124.4 %reduce-scatter.11.cloned.1.call-done = f32[24,2304]{1,0:T(8,128)} async-done(((f32[768,2304]{1,0:T(8,128)}), f32[24,2304]{1,0:T(8,128)}) %reduce-scatter.11.cloned.1.call-update) | async-done | bytes 221200 | tf_op jit(solution)/shard_map/reduce_scatter | solution.py:320
  720.3 353.0 %reduce-scatter.15.cloned.1.call-done = f32[4,24,3072]{2,1,0:T(8,128)} async-done(((f32[4,768,3072]{2,1,0:T(8,128)}), f32[4,24,3072]{2,1,0:T(8,128)}) %reduce-scatter.15.cloned.1.call-update) | async-done | bytes 1179664 | tf_op jit(solution)/shard_map/reduce_scatter | solution.py:322
  1073.3 353.9 %reduce-scatter.17.cloned.1.call-done = f32[4,96,768]{2,1,0:T(8,128)} async-done(((f32[4,3072,768]{2,1,0:T(8,128)}), f32[4,96,768]{2,1,0:T(8,128)}) %reduce-scatter.17.cloned.1.call-update) | async-done | bytes 1179664 | tf_op jit(solution)/shard_map/reduce_scatter | solution.py:323
  (218 shorter events, 110.7 us)
Async XLA Ops:
  7.2 66.6 %copy-start.15 = (bf16[1,128,768]{2,1,0:T(8,128)(2,1)S(1)}, bf16[1,128,768]{2,1,0:T(8,128)(2,1)}, u32[]{:S(2)}) copy-start(bf16[1,128,768]{2,1,0:T(8,128)(2,1)} %param.28) | copy-start | bytes 589828
  7.2 66.6 %copy-start.40 = (f32[768]{0:T(1024)S(1)}, f32[768]{0:T(1024)}, u32[]{:S(2)}) copy-start(f32[768]{0:T(1024)} %param.34) | copy-start | bytes 9220
  7.2 66.6 %all-gather.6.cloned.1.call-start = ((), (), s32[]{:S(2)}) async-start(), calls=%async_computation.6 | async-start | bytes 3649536 | tf_op jit(solution)/shard_map/all_gather | solution.py:94
  7.9 121.6 %all-gather.8.cloned.1.call-start = ((), (), s32[]{:S(2)}) async-start(), calls=%async_computation.7 | async-start | bytes 1216512 | tf_op jit(solution)/shard_map/all_gather | solution.py:95
  8.7 247.4 %all-gather.12.cloned.1.call-start = ((), (), s32[]{:S(2)}) async-start(), calls=%async_computation.9 | async-start | bytes 19464192 | tf_op jit(solution)/shard_map/all_gather | solution.py:97
  9.4 372.3 %all-gather.10.cloned.1.call-start = ((), (), s32[]{:S(2)}) async-start(), calls=%async_computation.8 | async-start | bytes 19464192 | tf_op jit(solution)/shard_map/all_gather | solution.py:96
  10.0 453.5 %reduce-scatter.21.cloned.1.call-start = ((), (), s32[]{:S(2)}) async-start(), calls=%async_computation.15 | async-start | bytes 983040
  14.5 62.1 %copy-start.23 = (bf16[4,96,128]{2,1,0:T(8,128)(2,1)}, bf16[4,96,128]{2,1,0:T(8,128)(2,1)S(1)}, u32[]{:S(2)}) copy-start(bf16[4,96,128]{2,1,0:T(8,128)(2,1)S(1)} %copy.119) | copy-start | bytes 294916
  22.0 54.6 %copy-start.48 = (f32[4,96]{1,0:T(4,128)}, f32[4,96]{1,0:T(4,128)S(1)}, u32[]{:S(2)}) copy-start(f32[4,96]{1,0:T(4,128)S(1)} %convolution_bitcast_fusion) | copy-start | bytes 4612
  23.1 53.5 %copy-start.46 = (f32[128]{0:T(128)}, f32[128]{0:T(128)S(1)}, u32[]{:S(2)}) copy-start(f32[128]{0:T(128)S(1)} %add_rsqrt_fusion.1) | copy-start | bytes 1540
  121.5 148.9 %copy-start.38 = (f32[12,128]{1,0:T(8,128)}, f32[12,128]{1,0:T(8,128)S(1)}, u32[]{:S(2)}) copy-start(f32[12,128]{1,0:T(8,128)S(1)} %get-tuple-element.1190) | copy-start | bytes 18436
  121.5 134.6 %copy-start.17 = (bf16[4,96,768]{2,1,0:T(8,128)(2,1)S(1)}, bf16[4,96,768]{2,1,0:T(8,128)(2,1)}, u32[]{:S(2)}) copy-start(bf16[4,96,768]{2,1,0:T(8,128)(2,1)} %fusion.47) | copy-start | bytes 1769476
  121.5 148.8 %copy-start.21 = (bf16[128,12,64]{0,2,1:T(8,128)(2,1)}, bf16[128,12,64]{0,2,1:T(8,128)(2,1)S(1)}, u32[]{:S(2)}) copy-start(bf16[128,12,64]{0,2,1:T(8,128)(2,1)S(1)} %convert_element_type.181) | copy-start | bytes 589828
  131.3 276.7 %copy-start.13 = (f32[128,768]{1,0:T(8,128)}, f32[128,768]{1,0:T(8,128)S(1)}, u32[]{:S(2)}) copy-start(f32[128,768]{1,0:T(8,128)S(1)} %get-tuple-element.752) | copy-start | bytes 1179652
  270.3 123.0 %copy-start.25 = (bf16[4,96,128]{2,1,0:T(8,128)(2,1)S(1)}, bf16[4,96,128]{2,1,0:T(8,128)(2,1)}, u32[]{:S(2)}) copy-start(bf16[4,96,128]{2,1,0:T(8,128)(2,1)} %copy-done.23) | copy-start | bytes 294916
  270.3 123.0 %copy-start.44 = (f32[768]{0:T(1024)S(1)}, f32[768]{0:T(1024)}, u32[]{:S(2)}) copy-start(f32[768]{0:T(1024)} %param.38) | copy-start | bytes 9220
  441.9 48.0 %reduce-scatter.19.cloned.1.call-start = ((), (), s32[]{:S(2)}) async-start(), calls=%async_computation.14 | async-start | bytes 983040
  444.3 46.7 %copy-start.16 = (bf16[1,128,768]{2,1,0:T(8,128)(2,1)S(1)}, bf16[1,128,768]{2,1,0:T(8,128)(2,1)}, u32[]{:S(2)}) copy-start(bf16[1,128,768]{2,1,0:T(8,128)(2,1)} %param.28) | copy-start | bytes 589828
  444.3 46.7 %copy-start.41 = (f32[768]{0:T(1024)S(1)}, f32[768]{0:T(1024)}, u32[]{:S(2)}) copy-start(f32[768]{0:T(1024)} %param.34) | copy-start | bytes 9220
  444.3 151.6 %reduce-scatter.13.cloned.1.call-start = ((), (), s32[]{:S(2)}) async-start(), calls=%async_computation.11 | async-start | bytes 2433024 | tf_op jit(solution)/shard_map/reduce_scatter | solution.py:321
  446.3 274.1 %reduce-scatter.11.cloned.1.call-start = ((), (), s32[]{:S(2)}) async-start(), calls=%async_computation.10 | async-start | bytes 7299072 | tf_op jit(solution)/shard_map/reduce_scatter | solution.py:320
  446.5 48.7 %copy-start.31 = (bf16[128,12,64]{0,2,1:T(8,128)(2,1)}, bf16[128,12,64]{0,2,1:T(8,128)(2,1)S(1)}, u32[]{:S(2)}) copy-start(bf16[128,12,64]{0,2,1:T(8,128)(2,1)S(1)} %convert_element_type.204) | copy-start | bytes 589828
  495.3 578.1 %reduce-scatter.15.cloned.1.call-start = ((), (), s32[]{:S(2)}) async-start(), calls=%async_computation.12 | async-start | bytes 38928384 | tf_op jit(solution)/shard_map/reduce_scatter | solution.py:322
  512.2 915.1 %reduce-scatter.17.cloned.1.call-start = ((), (), s32[]{:S(2)}) async-start(), calls=%async_computation.13 | async-start | bytes 38928384 | tf_op jit(solution)/shard_map/reduce_scatter | solution.py:323
  (36 other events, 266.9 us)
Sparse Core Ops, SparseCore 0:
  10.9 62.8 all-gather.5
  76.7 52.8 all-gather.7
  132.5 123.5 all-gather.11
  258.9 122.7 all-gather.9
  442.1 21.4 reduce-scatter.20
  466.7 23.2 reduce-scatter.18
  495.8 99.1 reduce-scatter.12
  602.2 118.0 reduce-scatter.10
  727.3 345.9 reduce-scatter.14
  1081.3 345.9 reduce-scatter.16
